TPU v7x, 256 devices: a whole 4x4x8 slice. The times are simulated.
256 devices in a mesh: layer: 16 (over y_lo, z), latent: 16 (over y_hi, x, core).
Axes of the slice: x: 4, y: 4 (y_hi: 2, y_lo: 2; y = y_hi * 2 + y_lo), z: 8, core: 2. Of those that a mesh axis runs over, the one named last changes fastest.
Arguments:
- layer_inputs: bfloat16 [384, 16384], P('latent', 'layer'), may hold values from -6 to 6
- mlp_outputs: bfloat16 [384, 16384], P('latent', 'layer'), may hold values from -6 to 6
- enc_weight: bfloat16 [16384, 4096], P('layer', 'latent'), may hold values from -0.125 to 0.125
- enc_bias: float32 [8, 4096], P(None, 'latent'), may hold values from -1 to 0.5
- dec_weight: bfloat16 [8, 4096, 16384], P(None, 'latent', 'layer'), may hold values from -0.03125 to 0.03125
Outputs:
- enc_grad: float32 [16384, 4096], P('layer', 'latent')
- dec_grad: bfloat16 [8, 4096, 16384], P(None, 'latent', 'layer')
All inputs are finite; a program needn't handle non-finite values.
Results may differ from a plain program's by a relative error of at most 0.011.
Values may be sent and summed in bfloat16 or wider, within the bound.
No kernel may reach another device: no remote copies, remote signals or barrier semaphores. Data moves between devices by JAX's collectives and lax.ppermute only.
A program may use at most 64 MiB of HBM per device.

v0:
```python
import jax
import jax.numpy as jnp
from jax import lax
from jax.sharding import PartitionSpec as P


def copy_for_each(x, axis):
    copies = jnp.broadcast_to(x, (lax.axis_size(axis), *x.shape))
    return lax.all_to_all(copies, axis, split_axis=0, concat_axis=0, tiled=True)


def joined_along(parts, dim):
    parts = jnp.moveaxis(parts, 0, dim)
    dims = parts.shape
    return parts.reshape(*dims[:dim], dims[dim] * dims[dim + 1], *dims[dim + 2 :])


def gathered_copies(x, axis, dim):
    parts = copy_for_each(x, axis)
    return joined_along(parts, dim)


def from_partner(x, axis, distance):
    return lax.ppermute(x, axis, [(i, i ^ 1 << distance) for i in range(lax.axis_size(axis))])


def in_blocks(x, dim, devices):
    dims = x.shape
    parts = x.reshape(*dims[:dim], devices, dims[dim] // devices, *dims[dim + 1 :])
    return jnp.moveaxis(parts, dim, 0)


def sent_and_summed(x, axis, dim):
    parts = in_blocks(x, dim, lax.axis_size(axis))
    arrived = lax.all_to_all(parts, axis, split_axis=0, concat_axis=0, tiled=True)
    return arrived.sum(axis=0)


def take_layer(stack, index):
    return lax.dynamic_index_in_dim(stack, index, 0, keepdims=False)


def local(layer_inputs, mlp_outputs, enc_weight, enc_bias, dec_weight):
    position = lax.axis_index("layer")
    layer_now = position // 2
    which_half = position % 2
    inputs_half = gathered_copies(layer_inputs, "latent", 0)
    total_rows = inputs_half.shape[0]
    half_rows = total_rows // 2
    width_half = dec_weight.shape[2]
    latent_cols = enc_weight.shape[1]
    own_part = jnp.dot(inputs_half, enc_weight, preferred_element_type=jnp.float32)
    partner = from_partner(own_part, "layer", 0)
    pre_acts = own_part + partner + take_layer(enc_bias, layer_now)[None, :]
    latents = jnp.maximum(pre_acts, 0.0).astype(jnp.bfloat16)
    own_rows = lax.dynamic_slice_in_dim(latents, which_half * half_rows, half_rows, 0)
    gathered = gathered_copies(own_rows[None], "layer", 0)
    layer_count = gathered.shape[0] // 2
    gathered = gathered.reshape(layer_count, total_rows, latent_cols)
    upper = layer_now + 1
    rscale = total_rows ** (-0.5)
    local_rows = mlp_outputs.shape[0]

    def add_source(source, total):
        block = take_layer(gathered, source)
        return total + jnp.dot(
            block, take_layer(dec_weight, source), preferred_element_type=jnp.float32
        )

    recon_own = sent_and_summed(
        lax.fori_loop(
            0,
            upper,
            add_source,
            jnp.zeros((local_rows * lax.axis_size("latent"), width_half), jnp.float32),
        ),
        "latent",
        0,
    )
    grad_own = ((recon_own - mlp_outputs.astype(jnp.float32)) * rscale).astype(jnp.bfloat16)
    out_grad = gathered_copies(grad_own, "latent", 0)

    def back_source(source, carry):
        grads, lat_terms = carry
        block = take_layer(gathered, source)
        weight = take_layer(dec_weight, source)
        dec_piece = lax.dot_general(
            block, out_grad, (((0,), (0,)), ((), ())), preferred_element_type=jnp.float32
        ).astype(jnp.bfloat16)
        lat_piece = lax.dot_general(
            out_grad, weight, (((1,), (1,)), ((), ())), preferred_element_type=jnp.float32
        )
        grads = lax.dynamic_update_index_in_dim(grads, dec_piece, source, 0)
        lat_terms = lax.dynamic_update_index_in_dim(lat_terms, lat_piece, source, 0)
        return (grads, lat_terms)

    start_carry = (
        jnp.zeros(dec_weight.shape, jnp.bfloat16),
        jnp.zeros((layer_count, total_rows, latent_cols), jnp.float32),
    )
    dec_grad, lat_terms = lax.fori_loop(0, upper, back_source, start_carry)
    lat_all = lax.psum(lat_terms, "layer")
    lat_grad = take_layer(lat_all, layer_now)
    pre_grad = jnp.where(pre_acts > 0.0, lat_grad, 0.0).astype(jnp.bfloat16)
    enc_grad = lax.dot_general(
        inputs_half, pre_grad, (((0,), (0,)), ((), ())), preferred_element_type=jnp.float32
    )
    return (enc_grad, dec_grad)


def solution(mesh):
    in_specs = (
        P("latent", "layer"),
        P("latent", "layer"),
        P("layer", "latent"),
        P(None, "latent"),
        P(None, "latent", "layer"),
    )
    out_specs = (P("layer", "latent"), P(None, "latent", "layer"))
    return jax.shard_map(local, mesh=mesh, in_specs=in_specs, out_specs=out_specs, check_vma=False)
```

profile of v0, /device:TPU:16, one launch (start us, length us, event | category | flops | bytes accessed | tf_op | source)
XLA Modules:
  0.0 270.2 jit_solution(17720900140261801250)
XLA Ops:
  0.6 0.0 copy-start
  0.6 0.9 broadcast_in_dim.30
  1.6 19.2 %all_to_all.20 = bf16[16,24,1024]{2,1,0:T(8,128)(2,1)S(1)} all-to-all(bf16[16,24,1024]{2,1,0:T(8,128)(2,1)S(1)} %broadcast_in_dim.30), channel_id=1, replica_groups=mesh['layer'=16,'latent'=16] {'latent'}, dimensions={0} | all-to-all | bytes 1572864 | tf_op jit(solution)/shard_map/all_to_all | solution.py:9
  20.8 0.0 copy-done
  20.8 0.4 fusion.19
  21.2 2.0 collective-permute-start
  23.2 0.7 constant_dynamic-slice_fusion.1
  23.9 8.7 %collective-permute-done = f32[384,256]{1,0:T(8,128)S(1)} collective-permute-done((f32[384,256]{1,0:T(8,128)S(1)}, f32[384,256]{1,0:T(8,128)S(1)}, u32[]{:S(2)}, u32[]{:S(2)}) %collective-permute-start) | collective-permute-done | bytes 393248 | tf_op jit(solution)/shard_map/ppermute | solution.py:24
  32.6 0.1 add_add_fusion
  32.7 1.3 broadcast_in_dim.33
  33.9 9.1 %all-to-all-start.1 = ((bf16[16,1,192,256]{3,2,1,0:T(8,128)(2,1)}), bf16[16,1,192,256]{3,2,1,0:T(8,128)(2,1)S(1)}, u32[]{:S(2)}, u32[]{:S(2)}) async-start(bf16[16,1,192,256]{3,2,1,0:T(8,128)(2,1)} %broadcast_in_dim.33), calls=%async_computation.1 | async-start | bytes 3145728 | tf_op jit(solution)/shard_map/all_to_all | solution.py:9
  43.1 37.2 %all-to-all-done.1 = bf16[16,1,192,256]{3,2,1,0:T(8,128)(2,1)S(1)} async-done(((bf16[16,1,192,256]{3,2,1,0:T(8,128)(2,1)}), bf16[16,1,192,256]{3,2,1,0:T(8,128)(2,1)S(1)}, u32[]{:S(2)}, u32[]{:S(2)}) %all-to-all-start.1) | async-done | bytes 1572896 | tf_op jit(solution)/shard_map/all_to_all | solution.py:9
  80.3 0.0 copy-start.1
  80.3 1.1 copy-done.1
  81.4 0.2 broadcast_in_dim.34
  81.6 1.6 while.22
  81.6 1.6 convolution_add_fusion.2
  83.3 0.0 copy-start.2
  83.3 26.6 %all_to_all.21 = f32[16,24,1024]{2,1,0:T(8,128)} all-to-all(f32[16,24,1024]{2,1,0:T(8,128)S(1)} %bitcast.56), channel_id=1, replica_groups=mesh['layer'=16,'latent'=16] {'latent'}, dimensions={0} | all-to-all | bytes 3145728 | tf_op jit(solution)/shard_map/all_to_all | solution.py:35
  109.8 1.5 reduce_sum.9
  111.3 0.0 copy-done.2
  111.4 1.0 broadcast_in_dim.35
  112.3 6.4 %all-to-all-start.3 = ((bf16[16,24,1024]{2,1,0:T(8,128)(2,1)}), bf16[16,24,1024]{2,1,0:T(8,128)(2,1)S(1)}, u32[]{:S(2)}, u32[]{:S(2)}) async-start(bf16[16,24,1024]{2,1,0:T(8,128)(2,1)} %broadcast_in_dim.35), calls=%async_computation.3 | async-start | bytes 1572864 | tf_op jit(solution)/shard_map/all_to_all | solution.py:9
  118.8 12.3 %all-to-all-done.3 = bf16[16,24,1024]{2,1,0:T(8,128)(2,1)S(1)} async-done(((bf16[16,24,1024]{2,1,0:T(8,128)(2,1)}), bf16[16,24,1024]{2,1,0:T(8,128)(2,1)S(1)}, u32[]{:S(2)}, u32[]{:S(2)}) %all-to-all-start.3) | async-done | bytes 786464 | tf_op jit(solution)/shard_map/all_to_all | solution.py:9
  131.1 1.9 broadcast_in_dim.32
  133.0 2.5 broadcast_in_dim.31
  135.5 4.4 %while.23 = (s32[]{:T(128)}, bf16[8,256,1024]{2,1,0:T(8,128)(2,1)}, f32[8,384,256]{1,2,0:T(8,128)}, s32[]{:T(128)}, bf16[8,384,256]{2,1,0:T(8,128)(2,1)}, /*inde...) while((s32[]{:T(128)}, bf16[8,256,1024]{2,1,0:T(8,128)(2,1)}, ...), condition=%wide.region_4.5_spmd, body=%wide.region_3.4_spmd.sunk | while | flops 402915328 | bytes 3213455 | solution.py:101
  135.5 2.2 fusion.40
  137.7 2.2 fusion.39
  139.9 128.3 %all-reduce.1 = bf16[8,384,256]{1,2,0:T(8,128)(2,1)S(1)} all-reduce(f32[8,384,256]{1,2,0:T(8,128)} %get-tuple-element.70), channel_id=1, replica_groups=mesh['layer'=16,'latent'=16] {'layer'}, use_global_device_ids=true, to_apply=%region_5.6 | all-reduce | flops 786432 | bytes 4718592 | tf_op jit(solution)/shard_map/psum | solution.py:102
  268.2 0.1 copy.9
  268.4 0.5 convolution_bitcast_fusion.1
  268.8 1.3 copy.10
  (3 shorter events, 0.1 us)
Async XLA Ops:
  0.6 20.2 %copy-start = (bf16[1024,256]{1,0:T(8,128)(2,1)S(1)}, bf16[1024,256]{1,0:T(8,128)(2,1)}, u32[]{:S(2)}) copy-start(bf16[1024,256]{1,0:T(8,128)(2,1)} %param.11) | copy-start | bytes 1572868
  21.2 11.4 %collective-permute-start = (f32[384,256]{1,0:T(8,128)S(1)}, f32[384,256]{1,0:T(8,128)S(1)}, u32[]{:S(2)}, u32[]{:S(2)}) collective-permute-start(f32[384,256]{1,0:T(8,128)S(1)} %fusion.19), channel_id=1, source_target_pairs={{0,16},{16,0},{32,48},{48,32},{64,80},{80,64},{96,112},{112,96},{1... | collective-permute-start | bytes 1179656 | tf_op jit(solution)/shard_map/ppermute | solution.py:24
  33.9 46.3 %all-to-all-start.1 = ((bf16[16,1,192,256]{3,2,1,0:T(8,128)(2,1)}), bf16[16,1,192,256]{3,2,1,0:T(8,128)(2,1)S(1)}, u32[]{:S(2)}, u32[]{:S(2)}) async-start(bf16[16,1,192,256]{3,2,1,0:T(8,128)(2,1)} %broadcast_in_dim.33), calls=%async_computation.1 | async-start | bytes 3145728 | tf_op jit(solution)/shard_map/all_to_all | solution.py:9
  80.3 1.1 copy-start.1
  83.3 28.1 %copy-start.2 = (bf16[24,1024]{1,0:T(8,128)(2,1)S(1)}, bf16[24,1024]{1,0:T(8,128)(2,1)}, u32[]{:S(2)}) copy-start(bf16[24,1024]{1,0:T(8,128)(2,1)} %param.10) | copy-start | bytes 147460
  112.3 18.7 %all-to-all-start.3 = ((bf16[16,24,1024]{2,1,0:T(8,128)(2,1)}), bf16[16,24,1024]{2,1,0:T(8,128)(2,1)S(1)}, u32[]{:S(2)}, u32[]{:S(2)}) async-start(bf16[16,24,1024]{2,1,0:T(8,128)(2,1)} %broadcast_in_dim.35), calls=%async_computation.3 | async-start | bytes 1572864 | tf_op jit(solution)/shard_map/all_to_all | solution.py:9
where the time goes:
time: 271 us; the launch traced here: 270 us
  blocking collectives  174 us (64%)
  waiting for transfers between devices  58.2 us (21%)
  starting transfers between devices  17.5 us (6%)
  local copies, waits for them, and re-layouts  11.2 us (4%)
  matrix products  6.84 us (3%)
    psum x1, blocking collectives, local(): lat_all = lax.psum(lat_terms, 'layer')  128 us
    all_to_all x2, waiting for transfers between devices, copy_for_each(): return lax.all_to_all(copies, axis, split_axis=0, concat_axis=0, tiled=True)  49.5 us
    all_to_all x1, blocking collectives, sent_and_summed(): lax.all_to_all(parts, axis, split_axis=0, concat_axis=0, tiled=True)  26.6 us
    all_to_all x1, blocking collectives, copy_for_each(): return lax.all_to_all(copies, axis, split_axis=0, concat_axis=0, tiled=True)  19.2 us
    all_to_all x2, starting transfers between devices, copy_for_each(): return lax.all_to_all(copies, axis, split_axis=0, concat_axis=0, tiled=True)  15.5 us
    ppermute x1, waiting for transfers between devices, from_partner(): lax.ppermute(x, axis, [(i, i ^ 1 << distance) for i in range(lax.axis_siz...  8.69 us
  transfers between devices with their start and end apart: 3, of which 3 were waited for; matrix products, arithmetic and copies ran while one was open for 0% of the time, Pallas kernels for 0%

commit v1 on v0

--- a/solution.py
+++ b/solution.py
@@ -2,6 +2,11 @@
 import jax.numpy as jnp
 from jax import lax
 from jax.sharding import PartitionSpec as P
+
+
+def summed_here(shard, axis):
+    parts = lax.all_gather(shard, axis)
+    return jnp.sum(parts, axis=0)
 
 
 def copy_for_each(x, axis):
@@ -99,7 +104,7 @@
         jnp.zeros((layer_count, total_rows, latent_cols), jnp.float32),
     )
     dec_grad, lat_terms = lax.fori_loop(0, upper, back_source, start_carry)
-    lat_all = lax.psum(lat_terms, "layer")
+    lat_all = summed_here(lat_terms, "layer")
     lat_grad = take_layer(lat_all, layer_now)
     pre_grad = jnp.where(pre_acts > 0.0, lat_grad, 0.0).astype(jnp.bfloat16)
     enc_grad = lax.dot_general(

time: 271 us -> 740 us (2.73)
  waiting for transfers between devices: 58.2 us -> 620 us
  blocking collectives: 174 us -> 45.8 us
  other arithmetic: 1.59 us -> 20.5 us
  between operations: 0.75 us -> 14.1 us
    all_gather x0 -> x1, waiting for transfers between devices: none -> 562 us  [summed_here(): parts = lax.all_gather(shard, axis)]
    psum x1 -> x0, blocking collectives: 128 us -> none  [local(): lat_all = lax.psum(lat_terms, 'layer')]
    reduce_sum x0 -> x1, other arithmetic: none -> 18.9 us  [summed_here(): return jnp.sum(parts, axis=0)]
  transfers between devices with their start and end apart: 3 -> 4, of which waited for: 3 -> 4; matrix products, arithmetic and copies ran while one was open for 0% -> 0% of each run, Pallas kernels for 0% -> 0%
where the time goes in v1:
time: 740 us; the launch traced here: 737 us
  waiting for transfers between devices  620 us (84%)
  blocking collectives  45.8 us (6%)
  other arithmetic  20.5 us (3%)
  starting transfers between devices  17.6 us (2%)
  between operations  14.1 us (2%)
  local copies, waits for them, and re-layouts  12 us (2%)
    all_gather x1, waiting for transfers between devices, summed_here(): parts = lax.all_gather(shard, axis)  562 us
    all_to_all x2, waiting for transfers between devices, copy_for_each(): return lax.all_to_all(copies, axis, split_axis=0, concat_axis=0, tiled=True)  49.5 us
    all_to_all x1, blocking collectives, sent_and_summed(): lax.all_to_all(parts, axis, split_axis=0, concat_axis=0, tiled=True)  26.6 us
    all_to_all x1, blocking collectives, copy_for_each(): return lax.all_to_all(copies, axis, split_axis=0, concat_axis=0, tiled=True)  19.2 us
    reduce_sum x1, other arithmetic, summed_here(): return jnp.sum(parts, axis=0)  18.9 us
    all_to_all x2, starting transfers between devices, copy_for_each(): return lax.all_to_all(copies, axis, split_axis=0, concat_axis=0, tiled=True)  15.5 us
  transfers between devices with their start and end apart: 4, of which 4 were waited for; matrix products, arithmetic and copies ran while one was open for 0% of the time, Pallas kernels for 0%

profile of v1, /device:TPU:16, one launch (start us, length us, event | category | flops | bytes accessed | tf_op | source)
XLA Modules:
  0.0 737.4 jit_solution(3842464875461008622)
XLA Ops:
  7.2 0.0 copy-start
  7.2 0.9 broadcast_in_dim.30
  8.1 19.2 %all_to_all.20 = bf16[16,24,1024]{2,1,0:T(8,128)(2,1)S(1)} all-to-all(bf16[16,24,1024]{2,1,0:T(8,128)(2,1)S(1)} %broadcast_in_dim.30), channel_id=1, replica_groups=mesh['layer'=16,'latent'=16] {'latent'}, dimensions={0} | all-to-all | bytes 1572864 | tf_op jit(solution)/shard_map/all_to_all | solution.py:14
  27.3 0.0 copy-done
  27.3 0.4 fusion.19
  27.7 2.0 collective-permute-start
  29.7 0.7 constant_dynamic-slice_fusion
  30.4 8.7 %collective-permute-done = f32[384,256]{1,0:T(8,128)S(1)} collective-permute-done((f32[384,256]{1,0:T(8,128)S(1)}, f32[384,256]{1,0:T(8,128)S(1)}, u32[]{:S(2)}, u32[]{:S(2)}) %collective-permute-start) | collective-permute-done | bytes 393248 | tf_op jit(solution)/shard_map/ppermute | solution.py:29
  39.1 0.1 add_add_fusion
  39.2 1.3 broadcast_in_dim.33
  40.5 9.1 %all-to-all-start.1 = ((bf16[16,1,192,256]{3,2,1,0:T(8,128)(2,1)}), bf16[16,1,192,256]{3,2,1,0:T(8,128)(2,1)S(1)}, u32[]{:S(2)}, u32[]{:S(2)}) async-start(bf16[16,1,192,256]{3,2,1,0:T(8,128)(2,1)} %broadcast_in_dim.33), calls=%async_computation.1 | async-start | bytes 3145728 | tf_op jit(solution)/shard_map/all_to_all | solution.py:14
  49.6 37.2 %all-to-all-done.1 = bf16[16,1,192,256]{3,2,1,0:T(8,128)(2,1)S(1)} async-done(((bf16[16,1,192,256]{3,2,1,0:T(8,128)(2,1)}), bf16[16,1,192,256]{3,2,1,0:T(8,128)(2,1)S(1)}, u32[]{:S(2)}, u32[]{:S(2)}) %all-to-all-start.1) | async-done | bytes 1572896 | tf_op jit(solution)/shard_map/all_to_all | solution.py:14
  86.8 0.0 copy-start.2
  86.8 1.1 copy-done.2
  88.0 0.2 broadcast_in_dim.34
  88.2 1.6 while.22
  88.2 1.6 convolution_add_fusion.2
  89.8 0.0 copy-start.3
  89.8 26.6 %all_to_all.21 = f32[16,24,1024]{2,1,0:T(8,128)} all-to-all(f32[16,24,1024]{2,1,0:T(8,128)S(1)} %bitcast.55), channel_id=1, replica_groups=mesh['layer'=16,'latent'=16] {'latent'}, dimensions={0} | all-to-all | bytes 3145728 | tf_op jit(solution)/shard_map/all_to_all | solution.py:40
  116.4 1.5 reduce_sum.18
  117.9 0.0 copy-done.3
  117.9 1.0 broadcast_in_dim.35
  118.9 6.4 all-to-all-start.3
  125.3 0.0 all-gather.3.cloned.1.call-start
  125.4 12.2 %all-to-all-done.3 = bf16[16,24,1024]{2,1,0:T(8,128)(2,1)S(1)} async-done(((bf16[16,24,1024]{2,1,0:T(8,128)(2,1)}), bf16[16,24,1024]{2,1,0:T(8,128)(2,1)S(1)}, u32[]{:S(2)}, u32[]{:S(2)}) %all-to-all-start.3) | async-done | bytes 786464 | tf_op jit(solution)/shard_map/all_to_all | solution.py:14
  137.6 1.9 broadcast_in_dim.32.clone
  139.5 2.5 broadcast_in_dim.31
  142.0 4.6 while.23
  142.0 1.5 convolution_bitcast_fusion.3
  143.5 0.2 copy.19
  143.7 0.8 constant_dynamic-update-slice_fusion.2
  144.5 2.2 fusion.38
  146.7 0.0 all-gather.3.cloned.1.call-update
  146.7 562.2 %all-gather.3.cloned.1.call-done = f32[128,384,256]{2,1,0:T(8,128)} async-done(((f32[8,384,256]{2,1,0:T(8,128)}), f32[128,384,256]{2,1,0:T(8,128)}) %all-gather.3.cloned.1.call-update) | async-done | bytes 50331664 | tf_op jit(solution)/shard_map/all_gather | solution.py:8
  708.9 0.0 copy-start.1
  708.9 18.9 %reduce_sum.19 = bf16[8,384,256]{2,1,0:T(8,128)(2,1)} reduce(f32[16,8,384,256]{3,2,1,0:T(8,128)} %bitcast.56, f32[]{:T(128)} %constant.75.clone.1), dimensions={0}, to_apply=%region_5.6 | reduce | flops 11796480 | bytes 51904516 | tf_op jit(solution)/shard_map/reduce_sum | solution.py:9
  727.8 1.4 convolution_bitcast_fusion.1
  729.2 1.3 copy.11
  730.5 0.0 copy-done.1
  (2 shorter events, 0.0 us)
Async XLA Ops:
  7.2 20.2 %copy-start = (bf16[1024,256]{1,0:T(8,128)(2,1)S(1)}, bf16[1024,256]{1,0:T(8,128)(2,1)}, u32[]{:S(2)}) copy-start(bf16[1024,256]{1,0:T(8,128)(2,1)} %param.11) | copy-start | bytes 1572868
  27.7 11.4 %collective-permute-start = (f32[384,256]{1,0:T(8,128)S(1)}, f32[384,256]{1,0:T(8,128)S(1)}, u32[]{:S(2)}, u32[]{:S(2)}) collective-permute-start(f32[384,256]{1,0:T(8,128)S(1)} %fusion.19), channel_id=1, source_target_pairs={{0,16},{16,0},{32,48},{48,32},{64,80},{80,64},{96,112},{112,96},{1... | collective-permute-start | bytes 1179656 | tf_op jit(solution)/shard_map/ppermute | solution.py:29
  40.5 46.3 %all-to-all-start.1 = ((bf16[16,1,192,256]{3,2,1,0:T(8,128)(2,1)}), bf16[16,1,192,256]{3,2,1,0:T(8,128)(2,1)S(1)}, u32[]{:S(2)}, u32[]{:S(2)}) async-start(bf16[16,1,192,256]{3,2,1,0:T(8,128)(2,1)} %broadcast_in_dim.33), calls=%async_computation.1 | async-start | bytes 3145728 | tf_op jit(solution)/shard_map/all_to_all | solution.py:14
  86.8 1.1 copy-start.2
  89.8 28.1 %copy-start.3 = (bf16[24,1024]{1,0:T(8,128)(2,1)S(1)}, bf16[24,1024]{1,0:T(8,128)(2,1)}, u32[]{:S(2)}) copy-start(bf16[24,1024]{1,0:T(8,128)(2,1)} %param.10) | copy-start | bytes 147460
  118.9 18.7 %all-to-all-start.3 = ((bf16[16,24,1024]{2,1,0:T(8,128)(2,1)}), bf16[16,24,1024]{2,1,0:T(8,128)(2,1)S(1)}, u32[]{:S(2)}, u32[]{:S(2)}) async-start(bf16[16,24,1024]{2,1,0:T(8,128)(2,1)} %broadcast_in_dim.35), calls=%async_computation.3 | async-start | bytes 1572864 | tf_op jit(solution)/shard_map/all_to_all | solution.py:14
  125.3 583.6 %all-gather.3.cloned.1.call-start = ((), (), s32[]{:S(2)}) async-start(), calls=%async_computation.4 | async-start | bytes 53477376 | tf_op jit(solution)/shard_map/all_gather | solution.py:8
  708.9 21.6 %copy-start.1 = (bf16[1024,256]{1,0:T(8,128)(2,1)S(1)}, bf16[1024,256]{1,0:T(8,128)(2,1)}, u32[]{:S(2)}) copy-start(bf16[1024,256]{1,0:T(8,128)(2,1)} %param.11) | copy-start | bytes 1572868
Sparse Core Ops, SparseCore 0:
  146.8 562.0 all-gather.2
